TPU v7x, 512 devices: a whole 4x4x16 slice. The times are simulated.
512 devices in a mesh: grp: 8 (over y, x_hi), comp: 64 (over x_lo, z, core).
Axes of the slice: x: 4 (x_hi: 2, x_lo: 2; x = x_hi * 2 + x_lo), y: 4, z: 16, core: 2. Of those that a mesh axis runs over, the one named last changes fastest.
Arguments:
- features: bfloat16 [1048576, 256], P(('grp', 'comp')), may hold values from -8 to 8
- means: float32 [1024, 256], P('comp'), may hold values from -1 to 1
- variances: float32 [1024, 256], P('comp'), may hold values from 0.5 to 2
- weight_logits: float32 [1024], replicated, may hold values from -1 to 1
Outputs:
- new_means: float32 [1024, 256], replicated
- new_variances: float32 [1024, 256], replicated
- new_log_weights: float32 [1024], replicated
- row_scores: float32 [1048576], P(('grp', 'comp'))
All inputs are finite; a program needn't handle non-finite values.
Results may differ from a plain program's by a relative error of at most 0.00085.
Values sent between devices are 32-bit elements; how exact they have to be, the bound alone decides.
A program may use at most 64 MiB of HBM per device.

v0:
```python
import math
import jax
import jax.numpy as jnp
from jax import lax
from jax.sharding import PartitionSpec as P


def update_step(moments, counts, total_rows):
    width = moments.shape[1] // 2
    denominator = (counts + 1.0)[:, None]
    fresh_means = moments[:, :width] / denominator
    fresh_variances = (moments[:, width:] + 1.0) / denominator - fresh_means * fresh_means + 0.01
    fresh_weights = jnp.log((counts + 1.0) / total_rows)
    return (fresh_means, fresh_variances, fresh_weights)


def on_device(features, means, variances, weight_logits):
    owned_count = means.shape[0]
    width = means.shape[1]
    first_owned = lax.axis_index("comp") * owned_count
    log_weights = lax.dynamic_slice_in_dim(
        jax.nn.log_softmax(weight_logits), first_owned, owned_count
    )
    inverse = 1.0 / variances
    coefficient = jnp.concatenate([-0.5 * inverse, means * inverse], axis=1)
    offsets = (
        log_weights
        - 0.5 * jnp.sum(jnp.log(variances) + means * means * inverse, axis=1)
        - 0.5 * width * math.log(2.0 * math.pi)
    )
    all_coefficient, all_offsets = (
        lax.all_gather(coefficient, "comp", axis=0, tiled=True),
        lax.all_gather(offsets, "comp", axis=0, tiled=True),
    )
    total_comps = all_coefficient.shape[0]
    local_rows = features.shape[0]
    block_size = min(512, local_rows)
    moments = jnp.zeros((total_comps, 2 * width), jnp.float32)
    counts = jnp.zeros((total_comps,), jnp.float32)
    score_pieces = []
    ones_row = jnp.ones((block_size,), jnp.bfloat16)
    for block_index in range(local_rows // block_size):
        block_rows = features[block_index * block_size : (block_index + 1) * block_size]
        values = block_rows.astype(jnp.float32)
        squared = values * values
        scores = (
            jnp.dot(
                jnp.concatenate([squared, values], axis=1),
                all_coefficient.T,
                precision=lax.Precision.HIGHEST,
            )
            + all_offsets
        )
        highest = jnp.max(scores, axis=1, keepdims=True)
        exponent = jnp.exp(scores - highest)
        totals = jnp.sum(exponent, axis=1, keepdims=True)
        responsibility = (exponent / totals).astype(jnp.bfloat16)
        score_pieces.append((highest[:, 0] + jnp.log(totals[:, 0])) / width)
        moment_inputs = jnp.concatenate([block_rows, squared.astype(jnp.bfloat16)], axis=1)
        moments = moments + jnp.dot(
            responsibility.T, moment_inputs, preferred_element_type=jnp.float32
        )
        counts = counts + jnp.dot(ones_row, responsibility, preferred_element_type=jnp.float32)
    row_scores = jnp.concatenate(score_pieces, axis=0)
    total_rows = jnp.float32(
        local_rows * lax.axis_size("grp") * lax.axis_size("comp") + total_comps
    )
    owned_moments, owned_counts = (
        lax.psum_scatter(moments, "comp", scatter_dimension=0, tiled=True),
        lax.psum_scatter(counts, "comp", scatter_dimension=0, tiled=True),
    )
    summed_moments, summed_counts = lax.psum((owned_moments, owned_counts), "grp")
    owned_means, owned_variances, owned_weights = update_step(
        summed_moments, summed_counts, total_rows
    )
    fresh_means, fresh_variances, fresh_weights = (
        lax.all_gather(owned_means, "comp", axis=0, tiled=True),
        lax.all_gather(owned_variances, "comp", axis=0, tiled=True),
        lax.all_gather(owned_weights, "comp", axis=0, tiled=True),
    )
    return (fresh_means, fresh_variances, fresh_weights, row_scores)


def solution(mesh):
    return jax.shard_map(
        on_device,
        mesh=mesh,
        in_specs=(P(("grp", "comp"), None), P("comp", None), P("comp", None), P()),
        out_specs=(P(), P(), P(), P(("grp", "comp"))),
        check_vma=False,
    )
```

profile of v0, /device:TPU:1, one launch (start us, length us, event | category | flops | bytes accessed | tf_op | source)
XLA Modules:
  0.0 667.8 jit_solution(7792017935220275641)
XLA Ops:
  7.2 0.9 add_reduce_fusion.4
  8.8 1.3 reduce_max.46
  10.1 1.9 exponential_reduce_fusion
  12.7 1.4 fusion.64
  14.7 1.3 subtract_subtract_fusion
  16.2 112.2 %all-reduce = f32[1024]{0:T(1024)S(1)} all-reduce(f32[1024]{0:T(1024)S(1)} %add_dynamic-update-slice_fusion), channel_id=1, replica_groups=mesh['grp'=8,'comp'=64] {'comp'}, use_global_device_ids=true, to_apply=%add | all-reduce | flops 1024 | bytes 8192
  128.4 2.3 fusion.63
  130.8 1.4 fusion.38
  132.2 5.9 all-gather.4.cloned.1.call-done
  138.0 5.5 fusion.4
  143.5 3.6 fusion.12
  147.1 3.7 add_reduce_fusion
  150.8 4.4 fusion.3
  155.3 1.5 fusion.1
  156.9 1.4 divide_convert_fusion.2
  161.3 2.1 add_add_fusion
  165.6 104.4 %all-reduce.2 = f32[1024]{0:T(1024)S(1)} all-reduce(f32[1024]{0:T(1024)S(1)} %add_add_fusion.1), channel_id=3, replica_groups=mesh['grp'=8,'comp'=64] {'comp'}, use_global_device_ids=true, to_apply=%region_13.14.clone | all-reduce | flops 1024 | bytes 8192
  270.1 114.1 %reduce-scatter.2.cloned.1.call-done = f32[16,512]{1,0:T(8,128)} async-done(((f32[1024,512]{1,0:T(8,128)}), f32[16,512]{1,0:T(8,128)}) %reduce-scatter.2.cloned.1.call-update) | async-done | bytes 32784 | tf_op jit(solution)/shard_map/reduce_scatter | solution.py:69
  384.2 35.4 %all-reduce.3 = (f32[16,512]{1,0:T(8,128)S(1)}, f32[16]{0:T(128)S(1)}) all-reduce(f32[16,512]{1,0:T(8,128)} %reduce-scatter.2.cloned.1.call-done, f32[16]{0:T(128)S(1)} %dynamic-slice.3), channel_id=1, replica_groups=mesh['grp'=8,'comp'=64] {'grp'}, use_global_device_ids=true, to_apply=%region_12.13 | all-reduce | flops 8208 | bytes 65664 | tf_op jit(solution)/shard_map/psum | solution.py:72
  421.6 115.8 %all-reduce.1 = f32[1024]{0:T(1024)} all-reduce(f32[1024]{0:T(1024)S(1)} %get-tuple-element.41), channel_id=1, replica_groups=mesh['grp'=8,'comp'=64] {'comp'}, use_global_device_ids=true, to_apply=%add.1 | all-reduce | flops 1024 | bytes 8192
  537.4 0.8 all-gather.6.cloned.1.call-done
  538.2 119.8 %all-gather.8.cloned.1.call-done = f32[1024,256]{1,0:T(8,128)} async-done(((f32[16,256]{1,0:T(8,128)}), f32[1024,256]{1,0:T(8,128)}) %all-gather.8.cloned.1.call-update) | async-done | bytes 1048592 | tf_op jit(solution)/shard_map/all_gather | solution.py:78
  658.0 2.4 copy.12
  660.3 1.0 copy.13
  (52 shorter events, 7.5 us)
Async XLA Ops:
  7.2 130.9 %all-gather.4.cloned.1.call-start = ((), (), s32[]{:S(2)}) async-start(), calls=%async_computation.1 | async-start | bytes 2129920 | tf_op jit(solution)/shard_map/all_gather | solution.py:32
  8.7 375.5 %reduce-scatter.2.cloned.1.call-start = ((), (), s32[]{:S(2)}) async-start(), calls=%async_computation.2 | async-start | bytes 2129920 | tf_op jit(solution)/shard_map/reduce_scatter | solution.py:69
  128.4 2.3 copy-start.3
  138.0 5.5 copy-start
  138.0 5.5 copy-start.4
  156.8 4.2 copy-start.1
  156.8 1.4 copy-start.8
  156.8 1.4 copy-start.11
  158.3 1.0 copy-start.6
  158.3 1.0 copy-start.10
  159.3 0.9 copy-start.5
  159.3 1.0 copy-start.9
  160.3 0.9 copy-start.7
  163.4 374.8 %all-gather.6.cloned.1.call-start = ((), (), s32[]{:S(2)}) async-start(), calls=%async_computation.3 | async-start | bytes 1064960 | tf_op jit(solution)/shard_map/all_gather | solution.py:77
  164.1 1.2 copy-start.2
  420.4 237.6 %all-gather.8.cloned.1.call-start = ((), (), s32[]{:S(2)}) async-start(), calls=%async_computation.4 | async-start | bytes 1064960 | tf_op jit(solution)/shard_map/all_gather | solution.py:78
  658.0 2.4 copy-start.12
Sparse Core Ops, SparseCore 0:
  10.2 127.8 all-gather.3
  163.5 220.5 reduce-scatter.1
  420.5 117.6 all-gather.5
  541.0 116.9 all-gather.7
where the time goes:
time: 669 us; the launch traced here: 668 us
  blocking collectives  368 us (55%)
  waiting for transfers between devices  241 us (36%)
  matrix products  22.6 us (3%)
  between operations  15.9 us (2%)
  other arithmetic  14.3 us (2%)
    unnamed x3, blocking collectives  332 us
    all_gather x1, waiting for transfers between devices, on_device(): lax.all_gather(owned_variances, 'comp', axis=0, tiled=True)  120 us
    reduce_scatter x1, waiting for transfers between devices, on_device(): lax.psum_scatter(moments, 'comp', scatter_dimension=0, tiled=True)  114 us
    psum x1, blocking collectives, on_device(): lax.psum((owned_moments, owned_counts), 'grp')  35.4 us
    dot_general x4, matrix products, on_device(): jnp.dot(jnp.concatenate([squared, values], axis=1), all_coefficient.T, pr...  17.2 us
  transfers between devices with their start and end apart: 4, of which 4 were waited for; matrix products, arithmetic and copies ran while one was open for 2% of the time, Pallas kernels for 0%

commit v1 on v0

--- a/solution.py
+++ b/solution.py
@@ -75,7 +75,10 @@
     )
     fresh_means, fresh_variances, fresh_weights = (
         lax.all_gather(owned_means, "comp", axis=0, tiled=True),
-        lax.all_gather(owned_variances, "comp", axis=0, tiled=True),
+        jnp.concatenate(
+            lax.all_to_all(jnp.stack([owned_variances] * lax.axis_size("comp")), "comp", 0, 0),
+            axis=0,
+        ),
         lax.all_gather(owned_weights, "comp", axis=0, tiled=True),
     )
     return (fresh_means, fresh_variances, fresh_weights, row_scores)

time: 669 us -> 592 us (0.88)
  waiting for transfers between devices: 241 us -> 121 us
  blocking collectives: 368 us -> 395 us
  starting transfers between devices: 0.16 us -> 15.3 us
    all_gather x1 -> x0, waiting for transfers between devices: 120 us -> none  [on_device(): lax.all_gather(owned_variances, 'comp', axis=0, tiled=True)]
    unnamed x3, blocking collectives: 332 us -> 360 us
    all_to_all x0 -> x1, starting transfers between devices: none -> 15.2 us  [on_device(): lax.all_to_all(jnp.stack([owned_variances] * lax.axis_size('comp')), 'com...]
  transfers between devices with their start and end apart: 4 -> 4, of which waited for: 4 -> 2; matrix products, arithmetic and copies ran while one was open for 2% -> 2% of each run, Pallas kernels for 0% -> 0%
where the time goes in v1:
time: 592 us; the launch traced here: 591 us
  blocking collectives  395 us (67%)
  waiting for transfers between devices  121 us (20%)
  matrix products  22.6 us (4%)
  between operations  15.9 us (3%)
  starting transfers between devices  15.3 us (3%)
  other arithmetic  14.3 us (2%)
  local copies, waits for them, and re-layouts  6.99 us (1%)
    unnamed x3, blocking collectives  360 us
    reduce_scatter x1, waiting for transfers between devices, on_device(): lax.psum_scatter(moments, 'comp', scatter_dimension=0, tiled=True)  114 us
    psum x1, blocking collectives, on_device(): lax.psum((owned_moments, owned_counts), 'grp')  35.3 us
    dot_general x4, matrix products, on_device(): jnp.dot(jnp.concatenate([squared, values], axis=1), all_coefficient.T, pr...  17.2 us
    all_to_all x1, starting transfers between devices, on_device(): lax.all_to_all(jnp.stack([owned_variances] * lax.axis_size('comp')), 'com...  15.2 us
  transfers between devices with their start and end apart: 4, of which 2 were waited for; matrix products, arithmetic and copies ran while one was open for 2% of the time, Pallas kernels for 0%

profile of v1, /device:TPU:1, one launch (start us, length us, event | category | flops | bytes accessed | tf_op | source)
XLA Modules:
  0.0 590.8 jit_solution(8780273197517670861)
XLA Ops:
  7.2 0.9 add_reduce_fusion.4
  8.8 1.3 reduce_max.46
  10.1 1.9 exponential_reduce_fusion
  12.7 1.4 fusion.64
  14.7 1.3 subtract_subtract_fusion
  16.2 112.2 %all-reduce = f32[1024]{0:T(1024)S(1)} all-reduce(f32[1024]{0:T(1024)S(1)} %add_dynamic-update-slice_fusion), channel_id=1, replica_groups=mesh['grp'=8,'comp'=64] {'comp'}, use_global_device_ids=true, to_apply=%add | all-reduce | flops 1024 | bytes 8192
  128.4 2.3 fusion.63
  130.8 1.4 fusion.38
  132.2 5.8 all-gather.3.cloned.1.call-done
  138.0 5.5 fusion.4
  143.5 3.6 fusion.12
  147.1 3.7 add_reduce_fusion
  150.8 4.4 fusion.3
  155.3 1.5 fusion.1
  156.9 1.4 divide_convert_fusion.2
  161.3 2.1 add_add_fusion
  165.5 104.4 %all-reduce.2 = f32[1024]{0:T(1024)S(1)} all-reduce(f32[1024]{0:T(1024)S(1)} %add_add_fusion.1), channel_id=3, replica_groups=mesh['grp'=8,'comp'=64] {'comp'}, use_global_device_ids=true, to_apply=%region_13.14.clone | all-reduce | flops 1024 | bytes 8192
  270.0 114.3 %reduce-scatter.2.cloned.1.call-done = f32[16,512]{1,0:T(8,128)} async-done(((f32[1024,512]{1,0:T(8,128)}), f32[16,512]{1,0:T(8,128)}) %reduce-scatter.2.cloned.1.call-update) | async-done | bytes 32784 | tf_op jit(solution)/shard_map/reduce_scatter | solution.py:69
  384.2 35.3 %all-reduce.3 = (f32[16,512]{1,0:T(8,128)S(1)}, f32[16]{0:T(128)S(1)}) all-reduce(f32[16,512]{1,0:T(8,128)} %reduce-scatter.2.cloned.1.call-done, f32[16]{0:T(128)S(1)} %dynamic-slice.3), channel_id=1, replica_groups=mesh['grp'=8,'comp'=64] {'grp'}, use_global_device_ids=true, to_apply=%region_12.13 | all-reduce | flops 8208 | bytes 65664 | tf_op jit(solution)/shard_map/psum | solution.py:72
  420.4 1.1 stack.2
  421.5 15.2 %all-to-all-start = ((f32[64,16,256]{2,1,0:T(8,128)}), f32[64,16,256]{2,1,0:T(8,128)S(1)}, u32[]{:S(2)}, u32[]{:S(2)}) async-start(f32[64,16,256]{2,1,0:T(8,128)} %stack.2), calls=%async_computation.1 | async-start | bytes 2097152 | tf_op jit(solution)/shard_map/all_to_all | solution.py:79
  438.0 143.0 %all-reduce.1 = f32[1024]{0:T(1024)} all-reduce(f32[1024]{0:T(1024)S(1)} %get-tuple-element.41), channel_id=1, replica_groups=mesh['grp'=8,'comp'=64] {'comp'}, use_global_device_ids=true, to_apply=%add.1 | all-reduce | flops 1024 | bytes 8192
  581.0 2.3 copy.12
  583.3 1.0 copy.13
  (50 shorter events, 7.6 us)
Async XLA Ops:
  7.2 130.9 %all-gather.3.cloned.1.call-start = ((), (), s32[]{:S(2)}) async-start(), calls=%async_computation.2 | async-start | bytes 2129920 | tf_op jit(solution)/shard_map/all_gather | solution.py:32
  8.7 375.5 %reduce-scatter.2.cloned.1.call-start = ((), (), s32[]{:S(2)}) async-start(), calls=%async_computation.3 | async-start | bytes 2129920 | tf_op jit(solution)/shard_map/reduce_scatter | solution.py:69
  128.4 2.3 copy-start.3
  138.0 5.5 copy-start
  138.0 5.5 copy-start.4
  156.8 4.2 copy-start.1
  156.8 1.4 copy-start.8
  156.8 1.4 copy-start.11
  158.3 1.0 copy-start.6
  158.3 1.0 copy-start.10
  159.3 0.9 copy-start.5
  159.3 1.0 copy-start.9
  160.3 0.9 copy-start.7
  164.0 1.2 copy-start.2
  421.5 159.6 %all-to-all-start = ((f32[64,16,256]{2,1,0:T(8,128)}), f32[64,16,256]{2,1,0:T(8,128)S(1)}, u32[]{:S(2)}, u32[]{:S(2)}) async-start(f32[64,16,256]{2,1,0:T(8,128)} %stack.2), calls=%async_computation.1 | async-start | bytes 2097152 | tf_op jit(solution)/shard_map/all_to_all | solution.py:79
  436.7 144.4 %all-gather.5.cloned.1.call-start = ((), (), s32[]{:S(2)}) async-start(), calls=%async_computation.4 | async-start | bytes 1064960 | tf_op jit(solution)/shard_map/all_gather | solution.py:77
Sparse Core Ops, SparseCore 0:
  10.2 127.8 all-gather.2
  163.5 220.6 reduce-scatter.1
  440.4 124.1 all-gather.4
